TPU v7x, 32 devices: a whole 2x2x4 slice. The times are simulated.
32 devices in a mesh: segment: 2 (over core), fsdp: 16 (over z, y, x).
Axes of the slice: x: 2, y: 2, z: 4, core: 2. Of those that a mesh axis runs over, the one named last changes fastest.
Arguments:
- inputs: bfloat16 [4, 48, 7, 7, 896], P(None, 'fsdp'), may hold values from -6 to 6
- cotangent: bfloat16 [4, 48, 7, 7, 896], P(None, 'fsdp'), may hold values from -6 to 6
- proj: bfloat16 [2, 896, 896], P('segment', 'fsdp'), may hold values from -0.1875 to 0.1875
- squeeze_weight: bfloat16 [2, 896, 224], P('segment', 'fsdp'), may hold values from -0.75 to 0.75
- excite_weight: bfloat16 [2, 224, 896], P('segment', None, 'fsdp'), may hold values from -0.75 to 0.75
Outputs:
- input_grads: bfloat16 [2, 4, 48, 7, 7, 896], P('segment', None, 'fsdp')
- proj_grads: float32 [2, 896, 896], P('segment', 'fsdp')
- squeeze_grads: float32 [2, 896, 224], P('segment', 'fsdp')
- excite_grads: float32 [2, 224, 896], P('segment', None, 'fsdp')
All inputs are finite; a program needn't handle non-finite values.
Results may differ from a plain program's by a relative error of at most 0.0054.
Values may be sent and summed in bfloat16 or wider, within the bound.
A program may use at most 64 MiB of HBM per device.

v0:
```python
import jax
import jax.numpy as jnp
from jax import lax
from jax.sharding import PartitionSpec as P

HIGH = lax.Precision.HIGHEST


def shifted(block, axis, distance):
    devices = range(lax.axis_size(axis))
    route = [(i - distance, i) for i in devices if i - distance in devices]
    return lax.ppermute(block, axis, route)


def silu_slope(value):
    sig = jax.nn.sigmoid(value)
    return sig * (1.0 + value * (1.0 - sig))


def gate_values(conv, squeeze, excite):
    pooled = jnp.mean(conv, axis=1)
    u_val = jnp.dot(pooled, squeeze.astype(jnp.float32), precision=HIGH)
    gate = jax.nn.sigmoid(jnp.dot(jax.nn.silu(u_val), excite.astype(jnp.float32), precision=HIGH))
    return (pooled, u_val, gate)


def run_forward(hin, weight, squeeze, excite):
    count, chans = (hin.shape[0], hin.shape[3])
    conv = jnp.dot(hin.reshape(-1, chans), weight, preferred_element_type=jnp.float32).reshape(
        count, -1, chans
    )
    pooled, u_val, gate = gate_values(conv, squeeze, excite)
    prod = conv * gate[:, None, :]
    out = (hin.reshape(count, -1, chans).astype(jnp.float32) + jax.nn.silu(prod)).astype(
        jnp.bfloat16
    )
    return (out.reshape(hin.shape), conv, pooled, u_val)


def run_backward(grad_in, hin, weight, squeeze, excite, conv, u_val):
    count, chans = (grad_in.shape[0], grad_in.shape[3])
    positions = conv.shape[1]
    z_val = jax.nn.silu(u_val)
    gate = jax.nn.sigmoid(jnp.dot(z_val, excite.astype(jnp.float32), precision=HIGH))
    prod = conv * gate[:, None, :]
    dyf = grad_in.reshape(count, positions, chans).astype(jnp.float32)
    dprod = dyf * silu_slope(prod)
    dgate = jnp.sum(dprod * conv, axis=1)
    dv_val = dgate * gate * (1.0 - gate)
    du_val = jnp.dot(dv_val, excite.astype(jnp.float32).T, precision=HIGH) * silu_slope(u_val)
    dpooled = jnp.dot(du_val, squeeze.astype(jnp.float32).T, precision=HIGH)
    dconv = (dprod * gate[:, None, :] + dpooled[:, None, :] / positions).astype(jnp.bfloat16)
    flat_d = dconv.reshape(-1, chans)
    back = lax.dot_general(
        flat_d, weight, (((1,), (1,)), ((), ())), preferred_element_type=jnp.float32
    )
    grad_out = (dyf.reshape(-1, chans) + back).astype(jnp.bfloat16).reshape(grad_in.shape)
    w_term = lax.dot_general(
        hin.reshape(-1, chans), flat_d, (((0,), (0,)), ((), ())), preferred_element_type=jnp.float32
    )
    return (grad_out, w_term, du_val, dv_val)


def store(buffer, value, index, valid):
    old = lax.dynamic_index_in_dim(buffer, index, 0, keepdims=False)
    return lax.dynamic_update_index_in_dim(buffer, jnp.where(valid, value, old), index, 0)


def fetch(buffer, index):
    return lax.dynamic_index_in_dim(buffer, index, 0, keepdims=False)


def body(inputs, cotangent, proj, squeeze_weight, excite_weight):
    segments = lax.axis_size("segment")
    here = lax.axis_index("segment")
    micro, batch, height, width, chans = inputs.shape
    inner = squeeze_weight.shape[2]
    positions = height * width
    full_proj, full_sq, full_ex = (
        lax.all_gather(proj, "fsdp", axis=1, tiled=True),
        lax.all_gather(squeeze_weight, "fsdp", axis=1, tiled=True),
        lax.all_gather(excite_weight, "fsdp", axis=2, tiled=True),
    )
    weight, squeeze, excite = (full_proj[0], full_sq[0], full_ex[0])
    act_shape = (micro, batch, height, width, chans)

    def forward_step(tick, incoming, fbufs):
        hin_buf, conv_buf, pool_buf, u_buf = fbufs
        index = tick - here
        valid = (index >= 0) & (index < micro)
        slot = jnp.clip(index, 0, micro - 1)
        feed = jnp.where(here == 0, fetch(inputs, slot), incoming)

        def forward_active(hin):
            return run_forward(hin, weight, squeeze, excite)

        def forward_resting(hin):
            return (
                jnp.zeros(hin.shape, jnp.bfloat16),
                jnp.zeros((batch, positions, chans), jnp.float32),
                jnp.zeros((batch, chans), jnp.float32),
                jnp.zeros((batch, inner), jnp.float32),
            )

        out, conv, pooled, u_val = lax.cond(valid, forward_active, forward_resting, feed)
        fbufs = (
            store(hin_buf, feed, slot, valid),
            store(conv_buf, conv, slot, valid),
            store(pool_buf, pooled, slot, valid),
            store(u_buf, u_val, slot, valid),
        )
        sent = shifted(out, "segment", 1)
        return (sent, fbufs)

    def backward_step(tick, offset, incoming, fbufs, bbufs):
        hin_buf, conv_buf, pool_buf, u_buf = fbufs
        grad_buf, du_buf, dv_buf, w_acc = bbufs
        index = tick - offset
        valid = (index >= 0) & (index < micro)
        slot = jnp.clip(index, 0, micro - 1)
        feed = jnp.where(here == segments - 1, fetch(cotangent, slot), incoming)
        hin = fetch(hin_buf, slot)
        conv = fetch(conv_buf, slot)
        pooled = fetch(pool_buf, slot)
        u_val = fetch(u_buf, slot)

        def backward_active(grad_in):
            return run_backward(grad_in, hin, weight, squeeze, excite, conv, u_val)

        def backward_resting(grad_in):
            return (
                jnp.zeros(grad_in.shape, jnp.bfloat16),
                jnp.zeros((chans, chans), jnp.float32),
                jnp.zeros((batch, inner), jnp.float32),
                jnp.zeros((batch, chans), jnp.float32),
            )

        grad_out, w_term, du_val, dv_val = lax.cond(valid, backward_active, backward_resting, feed)
        bbufs = (
            store(grad_buf, grad_out, slot, valid),
            store(du_buf, du_val, slot, valid),
            store(dv_buf, dv_val, slot, valid),
            w_acc + w_term,
        )
        sent = shifted(grad_out, "segment", -1)
        return (sent, bbufs)

    fstart = (
        jnp.zeros(act_shape, jnp.bfloat16),
        jnp.zeros((micro, batch, positions, chans), jnp.float32),
        jnp.zeros((micro, batch, chans), jnp.float32),
        jnp.zeros((micro, batch, inner), jnp.float32),
    )
    bstart = (
        jnp.zeros(act_shape, jnp.bfloat16),
        jnp.zeros((micro, batch, inner), jnp.float32),
        jnp.zeros((micro, batch, chans), jnp.float32),
        jnp.zeros((chans, chans), jnp.float32),
    )
    empty = jnp.zeros(act_shape[1:], jnp.bfloat16)
    ticks = micro + segments - 1

    def forward_tick(tick, carry):
        return forward_step(tick, carry[0], carry[1])

    _, fbufs = lax.fori_loop(0, ticks, forward_tick, (empty, fstart))

    def backward_tick(tick, carry):
        return backward_step(tick, segments - 1 - here, carry[0], fbufs, carry[1])

    _, bbufs = lax.fori_loop(0, ticks, backward_tick, (empty, bstart))
    grad_buf, du_buf, dv_buf, w_acc = bbufs
    pool_buf, u_buf = (fbufs[2], fbufs[3])
    proj_grads = lax.psum_scatter(w_acc[None], "fsdp", scatter_dimension=1, tiled=True)
    pool_flat = pool_buf.reshape(micro * batch, chans)
    z_flat = jax.nn.silu(u_buf.reshape(micro * batch, inner))
    du_flat = du_buf.reshape(micro * batch, inner)
    dv_flat = dv_buf.reshape(micro * batch, chans)
    sq_local = jnp.dot(pool_flat.T, du_flat, precision=HIGH)
    ex_local = jnp.dot(z_flat.T, dv_flat, precision=HIGH)
    sq_total, ex_total = lax.psum((sq_local, ex_local), "fsdp")
    share = chans // lax.axis_size("fsdp")
    begin = lax.axis_index("fsdp") * share
    sq_grads = lax.dynamic_slice_in_dim(sq_total, begin, share, 0)[None]
    ex_grads = lax.dynamic_slice_in_dim(ex_total, begin, share, 1)[None]
    return (grad_buf[None], proj_grads, sq_grads, ex_grads)


def solution(mesh):
    placed = (
        P(None, "fsdp", None, None, None),
        P(None, "fsdp", None, None, None),
        P("segment", "fsdp", None),
        P("segment", "fsdp", None),
        P("segment", None, "fsdp"),
    )
    return jax.shard_map(
        body,
        mesh=mesh,
        in_specs=placed,
        out_specs=(
            P("segment", None, "fsdp", None, None, None),
            P("segment", "fsdp", None),
            P("segment", "fsdp", None),
            P("segment", None, "fsdp"),
        ),
        check_vma=False,
    )
```

profile of v0, /device:TPU:0, one launch (start us, length us, event | category | flops | bytes accessed | tf_op | source)
XLA Modules:
  0.0 570.7 jit_solution(4285445937325981247)
XLA Ops:
  8.0 45.8 %all_gather.11 = bf16[1,224,896]{1,2,0:T(8,128)(2,1)S(1)} all-gather(bf16[1,224,56]{1,2,0:T(8,128)(2,1)} %param.17), channel_id=1, replica_groups=mesh['segment'=2,'fsdp'=16] {'fsdp'}, dimensions={2}, use_global_device_ids=true | all-gather | bytes 426496 | tf_op jit(solution)/shard_map/all_gather | solution.py:82
  57.4 41.2 %all_gather.10 = bf16[1,896,224]{2,1,0:T(8,128)(2,1)} all-gather(bf16[1,56,224]{2,1,0:T(8,128)(2,1)S(1)} %copy-done.11), channel_id=1, replica_groups=mesh['segment'=2,'fsdp'=16] {'fsdp'}, dimensions={1}, use_global_device_ids=true | all-gather | bytes 426496 | tf_op jit(solution)/shard_map/all_gather | solution.py:81
  101.4 74.4 %while.46 = (s32[]{:T(128)}, bf16[3,7,7,896]{3,2,1,0:T(8,128)(2,1)S(1)}, bf16[4,3,7,7,896]{4,3,2,1,0:T(8,128)(2,1)}, f32[4,3,49,896]{3,2,1,0:T(8,128)}, f32[4,3,...) while((s32[]{:T(128)}, ...), condition=%wide.region_4.5_spmd, body=%wide.region_0.4_spmd.sunk | while | flops 252073248 | bytes 11174111 | solution.py:166
  103.2 8.1 %conditional.5 = (bf16[3,7,7,896]{3,2,1,0:T(8,128)(2,1)S(1)}, f32[3,49,896]{2,1,0:T(8,128)}, f32[3,896]{1,0:T(4,128)}, f32[3,224]{1,0:T(4,128)}) conditional(s32[]{:T(128)} %convert_element_type.85, () %tuple.107, (bf16[3,7,7,896]{3,2,1,0:T(8,128)(2,1)S(1)}, bf16[896,896]{1,0:T(8,128)(2,1)}, bf16[896,224]{1,0:T(8,128)(2,1)}, ...), branch_computations={%region_1.1_spmd, %region_2.3_spmd} | conditional | flops 251674752 | bytes 5376032 | solution.py:105
  119.1 8.1 %conditional.5 = (bf16[3,7,7,896]{3,2,1,0:T(8,128)(2,1)S(1)}, f32[3,49,896]{2,1,0:T(8,128)}, f32[3,896]{1,0:T(4,128)}, f32[3,224]{1,0:T(4,128)}) conditional(s32[]{:T(128)} %convert_element_type.85, () %tuple.107, (bf16[3,7,7,896]{3,2,1,0:T(8,128)(2,1)S(1)}, bf16[896,896]{1,0:T(8,128)(2,1)}, bf16[896,224]{1,0:T(8,128)(2,1)}, ...), branch_computations={%region_1.1_spmd, %region_2.3_spmd} | conditional | flops 251674752 | bytes 5376032 | solution.py:105
  134.9 8.1 %conditional.5 = (bf16[3,7,7,896]{3,2,1,0:T(8,128)(2,1)S(1)}, f32[3,49,896]{2,1,0:T(8,128)}, f32[3,896]{1,0:T(4,128)}, f32[3,224]{1,0:T(4,128)}) conditional(s32[]{:T(128)} %convert_element_type.85, () %tuple.107, (bf16[3,7,7,896]{3,2,1,0:T(8,128)(2,1)S(1)}, bf16[896,896]{1,0:T(8,128)(2,1)}, bf16[896,224]{1,0:T(8,128)(2,1)}, ...), branch_computations={%region_1.1_spmd, %region_2.3_spmd} | conditional | flops 251674752 | bytes 5376032 | solution.py:105
  150.8 8.1 %conditional.5 = (bf16[3,7,7,896]{3,2,1,0:T(8,128)(2,1)S(1)}, f32[3,49,896]{2,1,0:T(8,128)}, f32[3,896]{1,0:T(4,128)}, f32[3,224]{1,0:T(4,128)}) conditional(s32[]{:T(128)} %convert_element_type.85, () %tuple.107, (bf16[3,7,7,896]{3,2,1,0:T(8,128)(2,1)S(1)}, bf16[896,896]{1,0:T(8,128)(2,1)}, bf16[896,224]{1,0:T(8,128)(2,1)}, ...), branch_computations={%region_1.1_spmd, %region_2.3_spmd} | conditional | flops 251674752 | bytes 5376032 | solution.py:105
  168.7 4.9 collective-permute-start
  179.0 172.5 %while.47 = (s32[]{:T(128)}, bf16[3,7,7,896]{3,2,1,0:T(8,128)(2,1)}, bf16[4,3,7,7,896]{4,3,2,1,0:T(8,128)(2,1)}, f32[4,3,224]{2,1,0:T(4,128)}, f32[4,3,896]{2,1,...) while((s32[]{:T(128)}, ...), condition=%wide.region_9.10_spmd.clone, body=%wide.region_5.9_spmd.clone.sunk | while | flops 500633504 | bytes 37965836 | solution.py:171
  187.5 21.6 %collective-permute-done.1 = bf16[3,7,7,896]{3,2,1,0:T(8,128)(2,1)} collective-permute-done((bf16[3,7,7,896]{3,2,1,0:T(8,128)(2,1)S(1)}, bf16[3,7,7,896]{3,2,1,0:T(8,128)(2,1)}, u32[]{:S(2)}, u32[]{:S(2)}) %collective-permute-start.1) | collective-permute-done | bytes 263456 | tf_op jit(solution)/shard_map/while/body/eval_jaxpr/ppermute | solution.py:12
  209.7 25.4 %conditional.6 = (bf16[3,7,7,896]{3,2,1,0:T(8,128)(2,1)S(1)}, f32[896,896]{1,0:T(8,128)S(1)}, f32[3,224]{1,0:T(4,128)S(1)}, f32[3,896]{1,0:T(4,128)S(1)}) conditional(s32[]{:T(128)} %convert_element_type.86, () %tuple.110, (pred[]{:T(512)}, bf16[4,3,7,7,896]{4,3,2,1,0:T(8,128)(2,1)}, s32[]{:T(128)}, bf16[3,7,7,896]{3,2,1,0:T(8,128)(2,1)}, ...), branch_computations={%region_6.6_spmd, %region_7.8_spmd} | conditional | flops 498892800 | bytes 25763420 | solution.py:138
  230.4 3.7 fusion.10
  239.0 3.9 select_add_fusion.2
  245.3 25.4 %conditional.6 = (bf16[3,7,7,896]{3,2,1,0:T(8,128)(2,1)S(1)}, f32[896,896]{1,0:T(8,128)S(1)}, f32[3,224]{1,0:T(4,128)S(1)}, f32[3,896]{1,0:T(4,128)S(1)}) conditional(s32[]{:T(128)} %convert_element_type.86, () %tuple.110, (pred[]{:T(512)}, bf16[4,3,7,7,896]{4,3,2,1,0:T(8,128)(2,1)}, s32[]{:T(128)}, bf16[3,7,7,896]{3,2,1,0:T(8,128)(2,1)}, ...), branch_computations={%region_6.6_spmd, %region_7.8_spmd} | conditional | flops 498892800 | bytes 25763420 | solution.py:138
  265.9 3.7 fusion.10
  274.6 3.9 select_add_fusion.2
  280.9 25.4 %conditional.6 = (bf16[3,7,7,896]{3,2,1,0:T(8,128)(2,1)S(1)}, f32[896,896]{1,0:T(8,128)S(1)}, f32[3,224]{1,0:T(4,128)S(1)}, f32[3,896]{1,0:T(4,128)S(1)}) conditional(s32[]{:T(128)} %convert_element_type.86, () %tuple.110, (pred[]{:T(512)}, bf16[4,3,7,7,896]{4,3,2,1,0:T(8,128)(2,1)}, s32[]{:T(128)}, bf16[3,7,7,896]{3,2,1,0:T(8,128)(2,1)}, ...), branch_computations={%region_6.6_spmd, %region_7.8_spmd} | conditional | flops 498892800 | bytes 25763420 | solution.py:138
  301.6 3.7 fusion.10
  310.2 3.9 select_add_fusion.2
  316.5 25.4 %conditional.6 = (bf16[3,7,7,896]{3,2,1,0:T(8,128)(2,1)S(1)}, f32[896,896]{1,0:T(8,128)S(1)}, f32[3,224]{1,0:T(4,128)S(1)}, f32[3,896]{1,0:T(4,128)S(1)}) conditional(s32[]{:T(128)} %convert_element_type.86, () %tuple.110, (pred[]{:T(512)}, bf16[4,3,7,7,896]{4,3,2,1,0:T(8,128)(2,1)}, s32[]{:T(128)}, bf16[3,7,7,896]{3,2,1,0:T(8,128)(2,1)}, ...), branch_computations={%region_6.6_spmd, %region_7.8_spmd} | conditional | flops 498892800 | bytes 25763420 | solution.py:138
  337.1 3.7 fusion.10
  345.8 3.9 select_add_fusion.2
  359.6 118.0 %all-reduce.4.cloned.1.call-done = (f32[896,224]{1,0:T(8,128)}, f32[224,896]{0,1:T(8,128)}) async-done(((f32[896,224]{1,0:T(8,128)}, f32[224,896]{0,1:T(8,128)}), (f32[896,224]{1,0:T(8,128)}, f32[224,896]{0,1:T(8,128)})) %all-reduce.4.cloned.1.call-update) | async-done | bytes 1605648 | tf_op jit(solution)/shard_map/psum | solution.py:181
  480.5 83.7 %reduce-scatter.6.cloned.1.call-done = f32[1,56,896]{2,1,0:T(8,128)} async-done(((f32[1,896,896]{2,1,0:T(8,128)}), f32[1,56,896]{2,1,0:T(8,128)}) %reduce-scatter.6.cloned.1.call-update) | async-done | bytes 200720
  (304 shorter events, 212.9 us)
Async XLA Ops:
  7.2 47.6 %copy-start.5 = (bf16[4,3,7,7,896]{4,0,3,2,1:T(4,128)(2,1)S(1)}, bf16[4,3,7,7,896]{4,0,3,2,1:T(4,128)(2,1)}, u32[]{:S(2)}) copy-start(bf16[4,3,7,7,896]{4,0,3,2,1:T(4,128)(2,1)} %param.13) | copy-start | bytes 3161092
  7.2 91.4 %all-gather.2.cloned.1.call-start = ((), (), s32[]{:S(2)}) async-start(), calls=%async_computation.1 | async-start | bytes 1705984 | tf_op jit(solution)/shard_map/all_gather | solution.py:80
  7.9 469.7 %all-reduce.4.cloned.1.call-start = ((), (), s32[]{:S(2)}) async-start(), calls=%async_computation.3 | async-start | bytes 3670016 | tf_op jit(solution)/shard_map/psum | solution.py:181
  111.3 5.9 %collective-permute-start = (bf16[3,7,7,896]{3,2,1,0:T(8,128)(2,1)S(1)}, bf16[3,7,7,896]{3,2,1,0:T(8,128)(2,1)S(1)}, u32[]{:S(2)}, u32[]{:S(2)}) collective-permute-start(bf16[3,7,7,896]{3,2,1,0:T(8,128)(2,1)S(1)} %get-tuple-element.1043), channel_id=1, source_target_pairs={{0,16},{1,17},{2,18},{3,19},{4,20},{5,21},{6,22},{7,23},{8,24},{9,... | collective-permute-start | bytes 790280 | tf_op jit(solution)/shard_map/while/body/eval_jaxpr/ppermute | solution.py:12
  127.2 5.9 %collective-permute-start = (bf16[3,7,7,896]{3,2,1,0:T(8,128)(2,1)S(1)}, bf16[3,7,7,896]{3,2,1,0:T(8,128)(2,1)S(1)}, u32[]{:S(2)}, u32[]{:S(2)}) collective-permute-start(bf16[3,7,7,896]{3,2,1,0:T(8,128)(2,1)S(1)} %get-tuple-element.1043), channel_id=1, source_target_pairs={{0,16},{1,17},{2,18},{3,19},{4,20},{5,21},{6,22},{7,23},{8,24},{9,... | collective-permute-start | bytes 790280 | tf_op jit(solution)/shard_map/while/body/eval_jaxpr/ppermute | solution.py:12
  143.0 5.9 %collective-permute-start = (bf16[3,7,7,896]{3,2,1,0:T(8,128)(2,1)S(1)}, bf16[3,7,7,896]{3,2,1,0:T(8,128)(2,1)S(1)}, u32[]{:S(2)}, u32[]{:S(2)}) collective-permute-start(bf16[3,7,7,896]{3,2,1,0:T(8,128)(2,1)S(1)} %get-tuple-element.1043), channel_id=1, source_target_pairs={{0,16},{1,17},{2,18},{3,19},{4,20},{5,21},{6,22},{7,23},{8,24},{9,... | collective-permute-start | bytes 790280 | tf_op jit(solution)/shard_map/while/body/eval_jaxpr/ppermute | solution.py:12
  158.9 5.9 %collective-permute-start = (bf16[3,7,7,896]{3,2,1,0:T(8,128)(2,1)S(1)}, bf16[3,7,7,896]{3,2,1,0:T(8,128)(2,1)S(1)}, u32[]{:S(2)}, u32[]{:S(2)}) collective-permute-start(bf16[3,7,7,896]{3,2,1,0:T(8,128)(2,1)S(1)} %get-tuple-element.1043), channel_id=1, source_target_pairs={{0,16},{1,17},{2,18},{3,19},{4,20},{5,21},{6,22},{7,23},{8,24},{9,... | collective-permute-start | bytes 790280 | tf_op jit(solution)/shard_map/while/body/eval_jaxpr/ppermute | solution.py:12
  168.7 7.1 %collective-permute-start = (bf16[3,7,7,896]{3,2,1,0:T(8,128)(2,1)S(1)}, bf16[3,7,7,896]{3,2,1,0:T(8,128)(2,1)S(1)}, u32[]{:S(2)}, u32[]{:S(2)}) collective-permute-start(bf16[3,7,7,896]{3,2,1,0:T(8,128)(2,1)S(1)} %get-tuple-element.1043), channel_id=1, source_target_pairs={{0,16},{1,17},{2,18},{3,19},{4,20},{5,21},{6,22},{7,23},{8,24},{9,... | collective-permute-start | bytes 790280 | tf_op jit(solution)/shard_map/while/body/eval_jaxpr/ppermute | solution.py:12
  179.8 29.3 %collective-permute-start.1 = (bf16[3,7,7,896]{3,2,1,0:T(8,128)(2,1)S(1)}, bf16[3,7,7,896]{3,2,1,0:T(8,128)(2,1)}, u32[]{:S(2)}, u32[]{:S(2)}) collective-permute-start(bf16[3,7,7,896]{3,2,1,0:T(8,128)(2,1)S(1)} %get-tuple-element.1063), channel_id=1, source_target_pairs={{16,0},{17,1},{18,2},{19,3},{20,4},{21,5},{22,6},{23,7},{24,8},{25... | collective-permute-start | bytes 790280 | tf_op jit(solution)/shard_map/while/body/eval_jaxpr/ppermute | solution.py:12
  183.8 25.4 %copy-start.9 = (f32[4,3,224]{2,1,0:T(4,128)S(1)}, f32[4,3,224]{2,1,0:T(4,128)}, u32[]{:S(2)}) copy-start(f32[4,3,224]{2,1,0:T(4,128)} %copy-done.8) | copy-start | bytes 32260 | tf_op jit(solution)/shard_map/while
  230.4 4.7 copy-start.7
  235.1 9.6 %collective-permute-start.1 = (bf16[3,7,7,896]{3,2,1,0:T(8,128)(2,1)S(1)}, bf16[3,7,7,896]{3,2,1,0:T(8,128)(2,1)}, u32[]{:S(2)}, u32[]{:S(2)}) collective-permute-start(bf16[3,7,7,896]{3,2,1,0:T(8,128)(2,1)S(1)} %get-tuple-element.1063), channel_id=1, source_target_pairs={{16,0},{17,1},{18,2},{19,3},{20,4},{21,5},{22,6},{23,7},{24,8},{25... | collective-permute-start | bytes 790280 | tf_op jit(solution)/shard_map/while/body/eval_jaxpr/ppermute | solution.py:12
  239.0 5.7 copy-start.9
  265.9 4.7 copy-start.4
  265.9 4.7 copy-start.7
  270.7 9.6 %collective-permute-start.1 = (bf16[3,7,7,896]{3,2,1,0:T(8,128)(2,1)S(1)}, bf16[3,7,7,896]{3,2,1,0:T(8,128)(2,1)}, u32[]{:S(2)}, u32[]{:S(2)}) collective-permute-start(bf16[3,7,7,896]{3,2,1,0:T(8,128)(2,1)S(1)} %get-tuple-element.1063), channel_id=1, source_target_pairs={{16,0},{17,1},{18,2},{19,3},{20,4},{21,5},{22,6},{23,7},{24,8},{25... | collective-permute-start | bytes 790280 | tf_op jit(solution)/shard_map/while/body/eval_jaxpr/ppermute | solution.py:12
  274.6 5.7 %copy-start.9 = (f32[4,3,224]{2,1,0:T(4,128)S(1)}, f32[4,3,224]{2,1,0:T(4,128)}, u32[]{:S(2)}) copy-start(f32[4,3,224]{2,1,0:T(4,128)} %copy-done.8) | copy-start | bytes 32260 | tf_op jit(solution)/shard_map/while
  301.6 4.7 copy-start.7
  306.3 9.6 %collective-permute-start.1 = (bf16[3,7,7,896]{3,2,1,0:T(8,128)(2,1)S(1)}, bf16[3,7,7,896]{3,2,1,0:T(8,128)(2,1)}, u32[]{:S(2)}, u32[]{:S(2)}) collective-permute-start(bf16[3,7,7,896]{3,2,1,0:T(8,128)(2,1)S(1)} %get-tuple-element.1063), channel_id=1, source_target_pairs={{16,0},{17,1},{18,2},{19,3},{20,4},{21,5},{22,6},{23,7},{24,8},{25... | collective-permute-start | bytes 790280 | tf_op jit(solution)/shard_map/while/body/eval_jaxpr/ppermute | solution.py:12
  310.2 5.7 copy-start.9
  337.1 4.7 copy-start.7
  341.9 9.6 %collective-permute-start.1 = (bf16[3,7,7,896]{3,2,1,0:T(8,128)(2,1)S(1)}, bf16[3,7,7,896]{3,2,1,0:T(8,128)(2,1)}, u32[]{:S(2)}, u32[]{:S(2)}) collective-permute-start(bf16[3,7,7,896]{3,2,1,0:T(8,128)(2,1)S(1)} %get-tuple-element.1063), channel_id=1, source_target_pairs={{16,0},{17,1},{18,2},{19,3},{20,4},{21,5},{22,6},{23,7},{24,8},{25... | collective-permute-start | bytes 790280 | tf_op jit(solution)/shard_map/while/body/eval_jaxpr/ppermute | solution.py:12
  345.8 5.7 copy-start.9
  356.9 207.3 %reduce-scatter.6.cloned.1.call-start = ((), (), s32[]{:S(2)}) async-start(), calls=%async_computation.2 | async-start | bytes 3411968
  (27 other events, 83.2 us)
Sparse Core Ops, SparseCore 0:
  10.7 63.2 all-gather.1
  357.0 120.5 all-reduce.3
  480.6 83.5 reduce-scatter.5
where the time goes:
time: 575 us; the launch traced here: 571 us
  waiting for transfers between devices  225 us (39%)
  local copies, waits for them, and re-layouts  93.5 us (16%)
  blocking collectives  87 us (15%)
  matrix products  68.5 us (12%)
  other arithmetic  65.6 us (11%)
  starting transfers between devices  16.7 us (3%)
  between operations  13.8 us (2%)
    psum x1, waiting for transfers between devices, body(): sq_total, ex_total = lax.psum((sq_local, ex_local), 'fsdp')  118 us
    unnamed x4, waiting for transfers between devices  85.1 us
    all_gather x1, blocking collectives, body(): lax.all_gather(excite_weight, 'fsdp', axis=2, tiled=True)  45.8 us
    all_gather x1, blocking collectives, body(): lax.all_gather(squeeze_weight, 'fsdp', axis=1, tiled=True)  41.2 us
    dynamic_update_slice x35, other arithmetic, store(): lax.dynamic_update_index_in_dim(buffer, jnp.where(valid, value, old), ind...  28.9 us
    dynamic_slice x35, local copies, waits for them, and re-layouts, store(): old = lax.dynamic_index_in_dim(buffer, index, 0, keepdims=False)  22.6 us
    ppermute x10, waiting for transfers between devices, shifted(): return lax.ppermute(block, axis, route)  21.6 us
    add x5, other arithmetic, backward_step(): w_acc + w_term  17.5 us
  transfers between devices with their start and end apart: 13, of which 3 were waited for; matrix products, arithmetic and copies ran while one was open for 12% of the time, Pallas kernels for 0%

commit v1 on v0

--- a/solution.py
+++ b/solution.py
@@ -1,6 +1,10 @@
+import functools
+
 import jax
 import jax.numpy as jnp
 from jax import lax
+from jax.experimental import pallas as pl
+from jax.experimental.pallas import tpu as pltpu
 from jax.sharding import PartitionSpec as P
 
 HIGH = lax.Precision.HIGHEST
@@ -186,6 +190,492 @@
     return (grad_buf[None], proj_grads, sq_grads, ex_grads)
 
 
+MESH = pl.DeviceIdType.MESH
+F32 = jnp.float32
+BF16 = jnp.bfloat16
+CHUNKS = 2
+PIX = 64
+GRP = 16
+
+
+def sigm(v):
+    return 0.5 * jnp.tanh(0.5 * v) + 0.5
+
+
+def halves(a):
+    hi = a.astype(BF16).astype(F32)
+    return hi, a - hi
+
+
+def dot_split(a, b, transposed):
+    rows = a.shape[0]
+    hi, lo = halves(a)
+    dims = (((1,), (1 if transposed else 0,)), ((), ()))
+    out = lax.dot_general(
+        jnp.concatenate([hi, lo], 0).astype(BF16), b, dims, preferred_element_type=F32
+    )
+    return out[:rows] + out[rows:]
+
+
+def outer_split(a, b):
+    ah, al = halves(a)
+    bh, bl = halves(b)
+    left = jnp.concatenate([ah, ah, al], 0).astype(BF16)
+    right = jnp.concatenate([bh, bl, bh], 0).astype(BF16)
+    return lax.dot_general(left, right, (((0,), (0,)), ((), ())), preferred_element_type=F32)
+
+
+def fused_kernel(
+    size, x_ref, cot_ref, a_ref, b_ref, gout_ref, pg_ref, sg_ref, eg_ref,
+    ga, gb, w_ref, sq_ref, ex_ref, hbuf, hnext, dybuf, conv, dpb, dconv,
+    pooled, u_s, gate_s, dgate, dpool, z_s, du_s, dv_s, wg,
+    sa, sb, rxa, rxb, rya, ryb, rza, rzb,
+    ag_send, ag_recv, rs_send, rs_recv, relay_send, relay_recv,
+):
+    zdim, share, images = size
+    chans = w_ref.shape[0]
+    cut = a_ref.shape[1] - sq_ref.shape[1]
+    seg = lax.axis_index("segment")
+    me = lax.axis_index("fsdp")
+    z, y, x = me // 4, (me // 2) % 2, me % 2
+    core = (1 - seg, me)
+
+    def place(zz, yy, xx):
+        return (seg, zz * 4 + yy * 2 + xx)
+
+    barrier = pltpu.get_barrier_semaphore()
+    pl.semaphore_signal(barrier, inc=1, device_id=core, device_id_type=MESH)
+    pl.semaphore_signal(barrier, inc=1, device_id=place(z, y, 1 - x), device_id_type=MESH)
+    pl.semaphore_signal(barrier, inc=1, device_id=place(z, 1 - y, x), device_id_type=MESH)
+    for step in range(1, zdim):
+        pl.semaphore_signal(
+            barrier, inc=1, device_id=place((z + step) % zdim, y, x), device_id_type=MESH
+        )
+    pl.semaphore_wait(barrier, 2 + zdim)
+
+    parts = ((0, ga, a_ref), (1, gb, b_ref))
+
+    def flip(part, minor):
+        if (part == 0) != minor:
+            return z, 1 - y, x
+        return z, y, 1 - x
+
+    def ag_copy(part, buf, block, kind, target, src=None):
+        return pltpu.make_async_remote_copy(
+            src_ref=buf.at[block] if src is None else src,
+            dst_ref=buf.at[block],
+            send_sem=ag_send.at[part, kind, block],
+            recv_sem=ag_recv.at[part, block],
+            device_id=target,
+            device_id_type=MESH,
+        )
+
+    def column(zz):
+        return zz * 4 + y * 2 + x
+
+    def first_block(part, zz):
+        return zz * 4 + ((1 - y) * 2 + x if part == 0 else y * 2 + (1 - x))
+
+    def second_block(part, zz):
+        return zz * 4 + (y * 2 + (1 - x) if part == 0 else (1 - y) * 2 + x)
+
+    def far_block(zz):
+        return zz * 4 + (1 - y) * 2 + (1 - x)
+
+    up, down = z + 1, z - 1
+
+    def spread(part, buf, zz, src=None):
+        block = column(zz)
+        ag_copy(part, buf, block, 2, place(*flip(part, False)), src).start()
+        ag_copy(part, buf, block, 3, place(*flip(part, True)), src).start()
+
+    for part, buf, own in parts:
+        block = column(z)
+
+        @pl.when(up < zdim)
+        def _(part=part, buf=buf, own=own, block=block):
+            ag_copy(part, buf, block, 0, place(up, y, x), own).start()
+
+        @pl.when(down >= 0)
+        def _(part=part, buf=buf, own=own, block=block):
+            ag_copy(part, buf, block, 1, place(down, y, x), own).start()
+
+        spread(part, buf, z, own)
+    for _, buf, own in parts:
+        buf[me] = own[...]
+
+    @pl.when(seg == 0)
+    def _():
+        hbuf[...] = x_ref[...]
+
+    @pl.when(seg == 1)
+    def _():
+        dybuf[...] = cot_ref[...]
+
+    pooled[...] = jnp.zeros_like(pooled)
+    dgate[...] = jnp.zeros_like(dgate)
+
+    def relay_first(part, buf, zz):
+        block = first_block(part, zz)
+        ag_copy(part, buf, block, 3, place(*flip(part, True))).wait_recv()
+        ag_copy(part, buf, block, 3, place(*flip(part, True))).start()
+
+    for part, buf, own in parts:
+        relay_first(part, buf, z)
+    for dist in range(1, zdim):
+        for part, buf, own in parts:
+
+            @pl.when(z - dist >= 0)
+            def _(part=part, buf=buf, dist=dist):
+                block = column(z - dist)
+                ag_copy(part, buf, block, 0, core).wait_recv()
+
+                @pl.when(up < zdim)
+                def _():
+                    ag_copy(part, buf, block, 0, place(up, y, x)).start()
+
+                spread(part, buf, z - dist)
+
+            @pl.when(z + dist < zdim)
+            def _(part=part, buf=buf, dist=dist):
+                block = column(z + dist)
+                ag_copy(part, buf, block, 1, core).wait_recv()
+
+                @pl.when(down >= 0)
+                def _():
+                    ag_copy(part, buf, block, 1, place(down, y, x)).start()
+
+                spread(part, buf, z + dist)
+
+        for part, buf, own in parts:
+
+            @pl.when(z - dist >= 0)
+            def _(part=part, buf=buf, dist=dist):
+                relay_first(part, buf, z - dist)
+
+            @pl.when(z + dist < zdim)
+            def _(part=part, buf=buf, dist=dist):
+                relay_first(part, buf, z + dist)
+
+    for part, buf, own in parts:
+        for zz in range(zdim):
+            ag_copy(part, buf, second_block(part, zz), 3, core).wait_recv()
+            ag_copy(part, buf, far_block(zz), 3, core).wait_recv()
+
+    def pack(k, _):
+        rows = pl.ds(pl.multiple_of(k * 2 * share, 2 * share), 2 * share)
+        pa = jnp.concatenate([ga[2 * k].astype(F32), ga[2 * k + 1].astype(F32)], 0).astype(BF16)
+        pb = jnp.concatenate([gb[2 * k].astype(F32), gb[2 * k + 1].astype(F32)], 0).astype(BF16)
+        w_ref[rows, :cut] = pa[:, :cut]
+        sq_ref[rows, :] = pa[:, cut:]
+        w_ref[rows, cut:] = pb[:, : chans - cut]
+        ex_ref[rows, :] = pb[:, chans - cut :]
+        return 0
+
+    lax.fori_loop(0, 2 * zdim, pack, 0)
+
+    def relay(src, dst, way, j):
+        return pltpu.make_async_remote_copy(
+            src_ref=src.at[j],
+            dst_ref=dst.at[j],
+            send_sem=relay_send.at[way, j],
+            recv_sem=relay_recv.at[way, j],
+            device_id=core,
+            device_id_type=MESH,
+        )
+
+    def rows_of(i, g):
+        return pl.ds(pl.multiple_of(i * PIX + g * GRP, GRP), GRP)
+
+    groups = PIX // GRP
+
+    def forward(j, _):
+        @pl.when(seg == 1)
+        def _():
+            relay(hnext, hbuf, 0, j).wait_recv()
+
+        conv[j] = jnp.dot(hbuf[j], w_ref[...], preferred_element_type=F32)
+
+        def pool(i, _):
+            acc = conv[j, rows_of(i, 0), :]
+            for g in range(1, groups):
+                acc = acc + conv[j, rows_of(i, g), :]
+            pooled[j, pl.ds(i, 1), :] = jnp.sum(acc, axis=0, keepdims=True) * (1.0 / 49.0)
+            return 0
+
+        lax.fori_loop(0, images, pool, 0)
+        u = dot_split(pooled[j], sq_ref[...], False)
+        u_s[j] = u
+        zv = u * sigm(u)
+        z_s[j] = zv
+        gate_s[j] = sigm(dot_split(zv, ex_ref[...], True))
+
+        @pl.when(seg == 0)
+        def _():
+            def emit(i, _):
+                g_row = gate_s[j, pl.ds(i, 1), :]
+                for g in range(groups):
+                    p = conv[j, rows_of(i, g), :] * g_row
+                    h = hbuf[j, rows_of(i, g), :].astype(F32)
+                    hnext[j, rows_of(i, g), :] = (h + p * sigm(p)).astype(BF16)
+                return 0
+
+            lax.fori_loop(0, images, emit, 0)
+            relay(hnext, hbuf, 0, j).start()
+
+        return 0
+
+    lax.fori_loop(0, CHUNKS, forward, 0)
+
+    def backward(j, _):
+        @pl.when(seg == 0)
+        def _():
+            relay(gout_ref, dybuf, 1, j).wait_recv()
+
+        def slope(i, _):
+            g_row = gate_s[j, pl.ds(i, 1), :]
+            total = jnp.zeros((GRP, chans), F32)
+            for g in range(groups):
+                c = conv[j, rows_of(i, g), :]
+                p = c * g_row
+                sig = sigm(p)
+                dp = dybuf[j, rows_of(i, g), :].astype(F32) * (sig * (1.0 + p * (1.0 - sig)))
+                total = total + dp * c
+                dpb[rows_of(i, g), :] = dp
+            dgate[pl.ds(i, 1), :] = jnp.sum(total, axis=0, keepdims=True)
+            return 0
+
+        lax.fori_loop(0, images, slope, 0)
+        gate = gate_s[j]
+        dv = dgate[...] * gate * (1.0 - gate)
+        dv_s[j] = dv
+        u = u_s[j]
+        sig = sigm(u)
+        du = dot_split(dv, ex_ref[...], False) * (sig * (1.0 + u * (1.0 - sig)))
+        du_s[j] = du
+        dpool[...] = dot_split(du, sq_ref[...], True) * (1.0 / 49.0)
+        spot = lax.broadcasted_iota(jnp.int32, (GRP, chans), 0)
+
+        def finish(i, _):
+            g_row = gate_s[j, pl.ds(i, 1), :]
+            d_row = dpool[pl.ds(i, 1), :]
+            for g in range(groups):
+                at = spot + g * GRP
+                keep = (at % 8 < 7) & (at < 56)
+                val = dpb[rows_of(i, g), :] * g_row + d_row
+                dconv[j, rows_of(i, g), :] = jnp.where(keep, val, 0.0).astype(BF16)
+            return 0
+
+        lax.fori_loop(0, images, finish, 0)
+        back = lax.dot_general(
+            dconv[j], w_ref[...], (((1,), (1,)), ((), ())), preferred_element_type=F32
+        )
+        gout_ref[j] = (dybuf[j].astype(F32) + back).astype(BF16)
+
+        @pl.when(seg == 1)
+        def _():
+            relay(gout_ref, dybuf, 1, j).start()
+
+        return 0
+
+    lax.fori_loop(0, CHUNKS, backward, 0)
+
+    total_rows = CHUNKS * images * PIX
+    flat_d = dconv[...].reshape(total_rows, chans)
+
+    def grad_rows(k, _):
+        cols = pl.ds(pl.multiple_of(k * 128, 128), 128)
+        h = hbuf[:, :, cols].reshape(total_rows, 128)
+        wg[pl.ds(pl.multiple_of(k * 128, 128), 128), :chans] = lax.dot_general(
+            h, flat_d, (((0,), (0,)), ((), ())), preferred_element_type=F32
+        )
+        return 0
+
+    lax.fori_loop(0, chans // 128, grad_rows, 0)
+    inner = sq_ref.shape[1]
+    small = CHUNKS * pooled.shape[1]
+    wg[:, chans : chans + inner] = outer_split(
+        pooled[...].reshape(small, chans), du_s[...].reshape(small, inner)
+    )
+    wg[:, chans + inner :] = outer_split(
+        dv_s[...].reshape(small, chans), z_s[...].reshape(small, inner)
+    )
+
+    def term(part, block):
+        rows = pl.ds(pl.multiple_of(block * share, 8), share)
+        if part == 0:
+            return wg[rows, :cut], wg[rows, chans : chans + inner]
+        return wg[rows, cut:chans], wg[rows, chans + inner :]
+
+    rs = ((0, sa, rxa, rya, rza), (1, sb, rxb, ryb, rzb))
+
+    def joined(part, block):
+        return jnp.concatenate(term(part, block), axis=1)
+
+    def rs_copy(part, src, dst, index, target):
+        return pltpu.make_async_remote_copy(
+            src_ref=src,
+            dst_ref=dst,
+            send_sem=rs_send.at[part, index],
+            recv_sem=rs_recv.at[part, index],
+            device_id=target,
+            device_id_type=MESH,
+        )
+
+    def z_at(k):
+        return (z + 1 + k) % zdim
+
+    def one(part, stage, r1, k, side):
+        zz = z_at(k)
+        block = far_block(zz) if side == 0 else second_block(part, zz)
+        return block, rs_copy(
+            part, stage.at[block], r1.at[2 * k + side], 2 * k + side, place(*flip(part, True))
+        )
+
+    def two(part, stage, r2, k):
+        block = first_block(part, z_at(k))
+        return block, rs_copy(
+            part, stage.at[block], r2.at[k], 2 * zdim + k, place(*flip(part, False))
+        )
+
+    def three(part, stage, r3, k):
+        block = column(z_at(k))
+        return block, rs_copy(
+            part, stage.at[block], r3.at[k], 3 * zdim + k, place(z_at(k), y, x)
+        )
+
+    for k in range(zdim):
+        for side in range(2):
+            for part, stage, r1, r2, r3 in rs:
+                block, copy = one(part, stage, r1, k, side)
+                stage[block] = joined(part, block).astype(BF16)
+                copy.start()
+    for k in range(zdim):
+        for part, stage, r1, r2, r3 in rs:
+            one(part, stage, r1, k, 0)[1].wait_recv()
+            block, copy = two(part, stage, r2, k)
+            stage[block] = (joined(part, block) + r1[2 * k].astype(F32)).astype(BF16)
+            copy.start()
+    for k in range(zdim):
+        for part, stage, r1, r2, r3 in rs:
+            one(part, stage, r1, k, 1)[1].wait_recv()
+            two(part, stage, r2, k)[1].wait_recv()
+            if k < zdim - 1:
+                block, copy = three(part, stage, r3, k)
+                value = joined(part, block) + r1[2 * k + 1].astype(F32) + r2[k].astype(F32)
+                stage[block] = value.astype(BF16)
+                copy.start()
+    last = zdim - 1
+    for part, stage, r1, r2, r3 in rs:
+        value = joined(part, me) + r1[2 * last + 1].astype(F32) + r2[last].astype(F32)
+        for k in range(zdim - 1):
+            three(part, stage, r3, k)[1].wait_recv()
+            value = value + r3[k].astype(F32)
+        if part == 0:
+            pg_ref[:, :cut] = value[:, :cut]
+            sg_ref[...] = value[:, cut:]
+        else:
+            pg_ref[:, cut:] = value[:, : chans - cut]
+            eg_ref[...] = value[:, chans - cut :]
+
+    for part, stage, r1, r2, r3 in rs:
+        for k in range(zdim):
+            one(part, stage, r1, k, 0)[1].wait_send()
+            one(part, stage, r1, k, 1)[1].wait_send()
+            two(part, stage, r2, k)[1].wait_send()
+            if k < zdim - 1:
+                three(part, stage, r3, k)[1].wait_send()
+    for part, buf, own in parts:
+        for zz in range(zdim):
+            ag_copy(part, buf, column(zz), 2, core).wait_send()
+            ag_copy(part, buf, column(zz), 3, core).wait_send()
+            ag_copy(part, buf, first_block(part, zz), 3, core).wait_send()
+
+            @pl.when((zz <= z) & (up < zdim))
+            def _(part=part, buf=buf, zz=zz):
+                ag_copy(part, buf, column(zz), 0, core).wait_send()
+
+            @pl.when((zz >= z) & (down >= 0))
+            def _(part=part, buf=buf, zz=zz):
+                ag_copy(part, buf, column(zz), 1, core).wait_send()
+
+    for j in range(CHUNKS):
+
+        @pl.when(seg == 0)
+        def _(j=j):
+            relay(hnext, hbuf, 0, j).wait_send()
+
+        @pl.when(seg == 1)
+        def _(j=j):
+            relay(gout_ref, dybuf, 1, j).wait_send()
+
+
+def fused_body(inputs, cotangent, proj, squeeze_weight, excite_weight):
+    fsdp = lax.axis_size("fsdp")
+    micro, batch, height, width, chans = inputs.shape
+    share, inner = squeeze_weight.shape[1:]
+    zdim = fsdp // 4
+    images = micro * batch // CHUNKS
+    rows = images * PIX
+    wide = -(-inner // 128) * 128
+    cut = (chans // 128 + 1) // 2 * 128
+    narrow = -(-images // 8) * 8
+
+    def padded(arr):
+        arr = jnp.pad(arr, ((0, 0), (0, 0), (0, 8 - height), (0, 8 - width), (0, 0)))
+        return arr.reshape(CHUNKS, rows, chans)
+
+    def widened(arr):
+        return jnp.pad(arr, ((0, 0), (0, wide - inner)))
+
+    part_a = jnp.concatenate([proj[0, :, :cut], widened(squeeze_weight[0])], 1)
+    part_b = jnp.concatenate([proj[0, :, cut:], widened(excite_weight[0].T)], 1)
+    ca, cb = part_a.shape[1], part_b.shape[1]
+    vm = pl.BlockSpec(memory_space=pltpu.VMEM)
+    v = pltpu.VMEM
+    dma = pltpu.SemaphoreType.DMA
+    act = v((CHUNKS, rows, chans), BF16)
+
+    def small(cols):
+        return v((CHUNKS, narrow, cols), F32)
+
+    gout, pg, sg, eg = pl.pallas_call(
+        functools.partial(fused_kernel, (zdim, share, images)),
+        out_shape=(
+            jax.ShapeDtypeStruct((CHUNKS, rows, chans), BF16),
+            jax.ShapeDtypeStruct((share, chans), F32),
+            jax.ShapeDtypeStruct((share, wide), F32),
+            jax.ShapeDtypeStruct((share, wide), F32),
+        ),
+        in_specs=[vm] * 4,
+        out_specs=(vm,) * 4,
+        scratch_shapes=[
+            v((fsdp, share, ca), BF16), v((fsdp, share, cb), BF16),
+            v((chans, chans), BF16), v((chans, wide), BF16), v((chans, wide), BF16),
+            act, act, act,
+            v((CHUNKS, rows, chans), F32), v((rows, chans), F32), act,
+            small(chans), small(wide), small(chans),
+            v((narrow, chans), F32), v((narrow, chans), F32),
+            small(wide), small(wide), small(chans),
+            v((chans, chans + 2 * wide), F32),
+            v((fsdp, share, ca), BF16), v((fsdp, share, cb), BF16),
+            v((2 * zdim, share, ca), BF16), v((2 * zdim, share, cb), BF16),
+            v((zdim, share, ca), BF16), v((zdim, share, cb), BF16),
+            v((zdim, share, ca), BF16), v((zdim, share, cb), BF16),
+            dma((2, 4, fsdp)), dma((2, fsdp)),
+            dma((2, 4 * zdim)), dma((2, 4 * zdim)),
+            dma((2, CHUNKS)), dma((2, CHUNKS)),
+        ],
+        compiler_params=pltpu.CompilerParams(collective_id=0, has_side_effects=True),
+    )(padded(inputs), padded(cotangent), part_a, part_b)
+    grads = gout.reshape(micro, batch, 8, 8, chans)[:, :, :height, :width]
+    return grads[None], pg[None], sg[None, :, :inner], eg[:, :inner].T[None]
+
+
+def suits(mesh):
+    return mesh.shape["segment"] == 2 and mesh.shape["fsdp"] == 16
+
+
 def solution(mesh):
     placed = (
         P(None, "fsdp", None, None, None),
@@ -195,7 +685,7 @@
         P("segment", None, "fsdp"),
     )
     return jax.shard_map(
-        body,
+        fused_body if suits(mesh) else body,
         mesh=mesh,
         in_specs=placed,
         out_specs=(

time: 575 us -> 93.9 us (0.16)
  waiting for transfers between devices: 225 us -> 0 us
  blocking collectives: 87 us -> 0 us
  local copies, waits for them, and re-layouts: 93.5 us -> 9.98 us
  Pallas kernels: 0 us -> 80 us
  matrix products: 68.5 us -> 0 us
  other arithmetic: 65.6 us -> 2.78 us
  starting transfers between devices: 16.7 us -> 0 us
  between operations: 13.8 us -> 0.69 us
    psum x1 -> x0, waiting for transfers between devices: 118 us -> none  [body(): sq_total, ex_total = lax.psum((sq_local, ex_local), 'fsdp')]
    all_gather x2 -> x0, blocking collectives: 87 us -> none  [the longest x1 45.8 us: body(): lax.all_gather(excite_weight, 'fsdp', axis=2, tiled=True)]
    unnamed x4 -> x0, waiting for transfers between devices: 85.1 us -> none
    pallas_call x0 -> x1, Pallas kernels: none -> 80 us  [fused_body(): pl.pallas_call(functools.partial(fused_kernel, (zdim, share, images)), ou...]
    dot_general x34 -> x0, matrix products: 68.5 us -> none  [the longest x4 14.7 us: run_backward(): lax.dot_general(flat_d, weight, (((1,), (1,)), ((), ())), preferred_eleme...]
    dynamic_update_slice x35 -> x0, other arithmetic: 28.9 us -> none  [store(): lax.dynamic_update_index_in_dim(buffer, jnp.where(valid, value, old), ind...]
    dynamic_slice x39 -> x0, local copies, waits for them, and re-layouts: 26.6 us -> none  [the longest x35 22.6 us: store(): old = lax.dynamic_index_in_dim(buffer, index, 0, keepdims=False)]
    ppermute x10 -> x0, waiting for transfers between devices: 21.6 us -> none  [shifted(): return lax.ppermute(block, axis, route)]
  transfers between devices with their start and end apart: 13 -> 0, of which waited for: 3 -> 0; matrix products, arithmetic and copies ran while one was open for 12% -> 0% of each run, Pallas kernels for 0% -> 0%
where the time goes in v1:
time: 93.9 us; the launch traced here: 93.4 us
  Pallas kernels  80 us (85%)
  local copies, waits for them, and re-layouts  9.98 us (11%)
  other arithmetic  2.78 us (3%)
    pallas_call x1, Pallas kernels, fused_body(): pl.pallas_call(functools.partial(fused_kernel, (zdim, share, images)), ou...  80 us
    unnamed x12, local copies, waits for them, and re-layouts  3.63 us
    pad x2, local copies, waits for them, and re-layouts, padded(): jnp.pad(arr, ((0, 0), (0, 0), (0, 8 - height), (0, 8 - width), (0, 0)))  2.71 us

profile of v1, /device:TPU:0, one launch (start us, length us, event | category | flops | bytes accessed | tf_op | source)
XLA Modules:
  0.0 93.4 jit_solution(4803684124187308199)
XLA Ops:
  0.6 0.8 slice_bitcast_fusion.3
  1.4 1.4 %fusion.3.b_ref = bf16[56,640]{1,0:T(8,128)(2,1)} fusion(bf16[56,224]{1,0:T(8,128)(2,1)} %bitcast.26, bf16[56,384]{1,0:T(8,128)(2,1)S(1)} %slice_bitcast_fusion.3), kind=kLoop, calls=%fused_computation.6 | loop fusion | flops 215040 | bytes 139776 | tf_op jit(solution)/shard_map/concatenate | solution.py:632
  2.8 0.8 slice_bitcast_fusion.2
  3.6 1.4 %fusion.2.a_ref = bf16[56,768]{1,0:T(8,128)(2,1)} fusion(bf16[56,224]{1,0:T(8,128)(2,1)} %bitcast.27, bf16[56,512]{1,0:T(8,128)(2,1)S(1)} %slice_bitcast_fusion.2), kind=kLoop, calls=%fused_computation.5 | loop fusion | flops 258048 | bytes 168448 | tf_op jit(solution)/shard_map/concatenate | solution.py:631
  5.0 1.4 %copy.13 = bf16[4,3,7,7,896]{4,3,2,1,0:T(8,128)(2,1)S(1)} copy(bf16[4,3,7,7,896]{4,0,3,2,1:T(4,128)(2,1)} %param.5) | data formatting | bytes 2107392
  6.4 0.0 copy-start
  6.4 1.4 %pad.14.clone = bf16[4,3,8,8,896]{4,3,2,1,0:T(8,128)(2,1)} pad(bf16[4,3,7,7,896]{4,3,2,1,0:T(8,128)(2,1)S(1)} %copy.13, bf16[]{:T(256)} %constant.2.clone.1), padding=0_0x0_0x0_1x0_1x0_0 | pad | bytes 2429954 | tf_op jit(solution)/shard_map/jit(_pad)/pad | solution.py:625
  7.8 0.0 copy-done
  7.8 0.2 copy.14
  7.9 1.3 %pad.15.clone = bf16[4,3,8,8,896]{4,3,2,1,0:T(8,128)(2,1)} pad(bf16[4,3,7,7,896]{4,3,2,1,0:T(8,128)(2,1)S(1)} %copy.14, bf16[]{:T(256)} %constant.2.clone.1), padding=0_0x0_0x0_1x0_1x0_0 | pad | bytes 2429954 | tf_op jit(solution)/shard_map/jit(_pad)/pad | solution.py:625
  9.3 80.0 %shard_map.84 = (bf16[2,384,896]{2,1,0:T(8,128)(2,1)}, f32[56,896]{1,0:T(8,128)}, f32[56,256]{1,0:T(8,128)}, f32[56,256]{1,0:T(8,128)}) custom-call(bf16[2,384,896]{2,1,0:T(8,128)(2,1)} %bitcast.21, bf16[2,384,896]{2,1,0:T(8,128)(2,1)} %bitcast.22, bf16[56,768]{1,0:T(8,128)(2,1)} %fusion.2.a_ref, bf16[56,640]{1,0:T(8,128)(2,1)} %fusion.3.b_ref), custom_call_target="tpu_custom_call" | custom-call | tf_op jit(solution)/shard_map/pallas_call | solution.py:642
  89.3 1.4 %slice.20 = bf16[4,3,7,7,896]{4,3,2,1,0:T(8,128)(2,1)S(1)} slice(bf16[4,3,8,8,896]{4,3,2,1,0:T(8,128)(2,1)} %bitcast.23), slice={[0:4], [0:3], [0:7], [0:7], [0:896]} | slice | bytes 2107392 | tf_op jit(solution)/shard_map/slice | solution.py:671
  90.7 0.0 copy-start.2
  90.7 0.0 copy-start.3
  90.7 0.0 copy-start.1
  90.7 1.4 %copy.16 = bf16[4,3,7,7,896]{4,0,3,2,1:T(4,128)(2,1)} copy(bf16[4,3,7,7,896]{4,3,2,1,0:T(8,128)(2,1)S(1)} %slice.20) | data formatting | bytes 2107392
  92.1 0.0 copy-done.2
  92.1 0.0 copy-done.3
  92.1 0.6 slice_bitcast_fusion
  92.8 0.0 copy-done.1
  92.8 0.7 copy.18
Async XLA Ops:
  6.4 1.4 %copy-start = (bf16[4,3,7,7,896]{4,0,3,2,1:T(4,128)(2,1)S(1)}, bf16[4,3,7,7,896]{4,0,3,2,1:T(4,128)(2,1)}, u32[]{:S(2)}) copy-start(bf16[4,3,7,7,896]{4,0,3,2,1:T(4,128)(2,1)} %param.6) | copy-start | bytes 3161092
  90.7 1.4 %copy-start.2 = (f32[56,256]{1,0:T(8,128)S(1)}, f32[56,256]{1,0:T(8,128)}, u32[]{:S(2)}) copy-start(f32[56,256]{1,0:T(8,128)} %get-tuple-element.10) | copy-start | bytes 172036
  90.7 1.4 %copy-start.3 = (f32[56,256]{1,0:T(8,128)S(1)}, f32[56,256]{1,0:T(8,128)}, u32[]{:S(2)}) copy-start(f32[56,256]{1,0:T(8,128)} %get-tuple-element.11) | copy-start | bytes 172036
  90.7 2.1 %copy-start.1 = (f32[56,896]{1,0:T(8,128)S(1)}, f32[56,896]{1,0:T(8,128)}, u32[]{:S(2)}) copy-start(f32[56,896]{1,0:T(8,128)} %get-tuple-element.9) | copy-start | bytes 602116

commit v2 on v1

--- a/solution.py
+++ b/solution.py
@@ -193,8 +193,6 @@
 MESH = pl.DeviceIdType.MESH
 F32 = jnp.float32
 BF16 = jnp.bfloat16
-CHUNKS = 2
-PIX = 64
 GRP = 16
 
 
@@ -218,6 +216,9 @@
 
 
 def outer_split(a, b):
+    fill = -a.shape[0] % GRP
+    a = jnp.concatenate([a, jnp.zeros((fill, a.shape[1]), F32)], 0)
+    b = jnp.concatenate([b, jnp.zeros((fill, b.shape[1]), F32)], 0)
     ah, al = halves(a)
     bh, bl = halves(b)
     left = jnp.concatenate([ah, ah, al], 0).astype(BF16)
@@ -228,11 +229,14 @@
 def fused_kernel(
     size, x_ref, cot_ref, a_ref, b_ref, gout_ref, pg_ref, sg_ref, eg_ref,
     ga, gb, w_ref, sq_ref, ex_ref, hbuf, hnext, dybuf, conv, dpb, dconv,
-    pooled, u_s, gate_s, dgate, dpool, z_s, du_s, dv_s, wg,
+    pooled, u_s, gate_s, dpool, z_s, du_s, dv_s, wg,
     sa, sb, rxa, rxb, rya, ryb, rza, rzb,
     ag_send, ag_recv, rs_send, rs_recv, relay_send, relay_recv,
 ):
-    zdim, share, images = size
+    zdim, share = size
+    chunks, positions, micro, _ = x_ref.shape
+    rows = hbuf.shape[1]
+    packs = rows // GRP
     chans = w_ref.shape[0]
     cut = a_ref.shape[1] - sq_ref.shape[1]
     seg = lax.axis_index("segment")
@@ -304,16 +308,39 @@
     for _, buf, own in parts:
         buf[me] = own[...]
 
+    def rows_of(q):
+        return pl.ds(pl.multiple_of(q * GRP, GRP), GRP)
+
+    def load(src, dst):
+        step = GRP // micro
+
+        def one_chunk(j, _):
+            def group(q, _):
+                four = [src[j, q * step + t].astype(F32) for t in range(step)]
+                dst[j, rows_of(q), :] = jnp.concatenate(four, 0).astype(BF16)
+                return 0
+
+            lax.fori_loop(0, positions // step, group, 0)
+            for q in range(positions // step, packs):
+                four = [
+                    src[j, q * step + t].astype(F32)
+                    if q * step + t < positions
+                    else jnp.zeros((micro, chans), F32)
+                    for t in range(step)
+                ]
+                dst[j, q * GRP : (q + 1) * GRP, :] = jnp.concatenate(four, 0).astype(BF16)
+            return 0
+
+        lax.fori_loop(0, chunks, one_chunk, 0)
+
     @pl.when(seg == 0)
     def _():
-        hbuf[...] = x_ref[...]
+        load(x_ref, hbuf)
 
     @pl.when(seg == 1)
     def _():
-        dybuf[...] = cot_ref[...]
-
-    pooled[...] = jnp.zeros_like(pooled)
-    dgate[...] = jnp.zeros_like(dgate)
+        load(cot_ref, dybuf)
+
 
     def relay_first(part, buf, zz):
         block = first_block(part, zz)
@@ -363,13 +390,13 @@
             ag_copy(part, buf, far_block(zz), 3, core).wait_recv()
 
     def pack(k, _):
-        rows = pl.ds(pl.multiple_of(k * 2 * share, 2 * share), 2 * share)
+        at = pl.ds(pl.multiple_of(k * 2 * share, 2 * share), 2 * share)
         pa = jnp.concatenate([ga[2 * k].astype(F32), ga[2 * k + 1].astype(F32)], 0).astype(BF16)
         pb = jnp.concatenate([gb[2 * k].astype(F32), gb[2 * k + 1].astype(F32)], 0).astype(BF16)
-        w_ref[rows, :cut] = pa[:, :cut]
-        sq_ref[rows, :] = pa[:, cut:]
-        w_ref[rows, cut:] = pb[:, : chans - cut]
-        ex_ref[rows, :] = pb[:, chans - cut :]
+        w_ref[at, :cut] = pa[:, :cut]
+        sq_ref[at, :] = pa[:, cut:]
+        w_ref[at, cut:] = pb[:, : chans - cut]
+        ex_ref[at, :] = pb[:, chans - cut :]
         return 0
 
     lax.fori_loop(0, 2 * zdim, pack, 0)
@@ -384,10 +411,15 @@
             device_id_type=MESH,
         )
 
-    def rows_of(i, g):
-        return pl.ds(pl.multiple_of(i * PIX + g * GRP, GRP), GRP)
-
-    groups = PIX // GRP
+    real = lax.broadcasted_iota(jnp.int32, (8, chans), 0) < micro
+
+    def fold(acc):
+        both = acc[:8] + acc[8:]
+        return jnp.where(real, both + pltpu.roll(both, micro, 0), 0.0)
+
+    def twice(v):
+        v = jnp.where(real, v, 0.0)
+        return v + pltpu.roll(v, micro, 0)
 
     def forward(j, _):
         @pl.when(seg == 1)
@@ -396,77 +428,66 @@
 
         conv[j] = jnp.dot(hbuf[j], w_ref[...], preferred_element_type=F32)
 
-        def pool(i, _):
-            acc = conv[j, rows_of(i, 0), :]
-            for g in range(1, groups):
-                acc = acc + conv[j, rows_of(i, g), :]
-            pooled[j, pl.ds(i, 1), :] = jnp.sum(acc, axis=0, keepdims=True) * (1.0 / 49.0)
-            return 0
-
-        lax.fori_loop(0, images, pool, 0)
-        u = dot_split(pooled[j], sq_ref[...], False)
+        def pool(q, acc):
+            return acc + conv[j, rows_of(q), :]
+
+        total = lax.fori_loop(0, packs, pool, jnp.zeros((GRP, chans), F32))
+        mean = fold(total) * (1.0 / positions)
+        pooled[j] = mean
+        u = dot_split(mean, sq_ref[...], False)
         u_s[j] = u
         zv = u * sigm(u)
         z_s[j] = zv
-        gate_s[j] = sigm(dot_split(zv, ex_ref[...], True))
+        gate = twice(sigm(dot_split(zv, ex_ref[...], True)))
+        gate_s[j] = jnp.concatenate([gate, gate], 0)
 
         @pl.when(seg == 0)
         def _():
-            def emit(i, _):
-                g_row = gate_s[j, pl.ds(i, 1), :]
-                for g in range(groups):
-                    p = conv[j, rows_of(i, g), :] * g_row
-                    h = hbuf[j, rows_of(i, g), :].astype(F32)
-                    hnext[j, rows_of(i, g), :] = (h + p * sigm(p)).astype(BF16)
+            def emit(q, _):
+                p = conv[j, rows_of(q), :] * gate_s[j]
+                h = hbuf[j, rows_of(q), :].astype(F32)
+                hnext[j, rows_of(q), :] = (h + p * sigm(p)).astype(BF16)
                 return 0
 
-            lax.fori_loop(0, images, emit, 0)
+            lax.fori_loop(0, packs, emit, 0)
             relay(hnext, hbuf, 0, j).start()
 
         return 0
 
-    lax.fori_loop(0, CHUNKS, forward, 0)
+    lax.fori_loop(0, chunks, forward, 0)
 
     def backward(j, _):
         @pl.when(seg == 0)
         def _():
             relay(gout_ref, dybuf, 1, j).wait_recv()
 
-        def slope(i, _):
-            g_row = gate_s[j, pl.ds(i, 1), :]
-            total = jnp.zeros((GRP, chans), F32)
-            for g in range(groups):
-                c = conv[j, rows_of(i, g), :]
-                p = c * g_row
-                sig = sigm(p)
-                dp = dybuf[j, rows_of(i, g), :].astype(F32) * (sig * (1.0 + p * (1.0 - sig)))
-                total = total + dp * c
-                dpb[rows_of(i, g), :] = dp
-            dgate[pl.ds(i, 1), :] = jnp.sum(total, axis=0, keepdims=True)
-            return 0
-
-        lax.fori_loop(0, images, slope, 0)
-        gate = gate_s[j]
-        dv = dgate[...] * gate * (1.0 - gate)
+        def slope(q, total):
+            c = conv[j, rows_of(q), :]
+            p = c * gate_s[j]
+            sig = sigm(p)
+            dp = dybuf[j, rows_of(q), :].astype(F32) * (sig * (1.0 + p * (1.0 - sig)))
+            dpb[rows_of(q), :] = dp
+            return total + dp * c
+
+        total = lax.fori_loop(0, packs, slope, jnp.zeros((GRP, chans), F32))
+        gate = gate_s[j, :8]
+        dv = fold(total) * gate * (1.0 - gate)
         dv_s[j] = dv
         u = u_s[j]
         sig = sigm(u)
         du = dot_split(dv, ex_ref[...], False) * (sig * (1.0 + u * (1.0 - sig)))
         du_s[j] = du
-        dpool[...] = dot_split(du, sq_ref[...], True) * (1.0 / 49.0)
+        spread_d = twice(dot_split(du, sq_ref[...], True)) * (1.0 / positions)
+        dpool[...] = jnp.concatenate([spread_d, spread_d], 0)
         spot = lax.broadcasted_iota(jnp.int32, (GRP, chans), 0)
 
-        def finish(i, _):
-            g_row = gate_s[j, pl.ds(i, 1), :]
-            d_row = dpool[pl.ds(i, 1), :]
-            for g in range(groups):
-                at = spot + g * GRP
-                keep = (at % 8 < 7) & (at < 56)
-                val = dpb[rows_of(i, g), :] * g_row + d_row
-                dconv[j, rows_of(i, g), :] = jnp.where(keep, val, 0.0).astype(BF16)
+        def finish(q, _):
+            val = dpb[rows_of(q), :] * gate_s[j] + dpool[...]
+            keep = spot + q * GRP < positions * micro
+            dconv[j, rows_of(q), :] = jnp.where(keep, val, 0.0).astype(BF16)
             return 0
 
-        lax.fori_loop(0, images, finish, 0)
+        lax.fori_loop(0, packs, finish, 0)
         back = lax.dot_general(
             dconv[j], w_ref[...], (((1,), (1,)), ((), ())), preferred_element_type=F32
         )
@@ -478,9 +499,9 @@
 
         return 0
 
-    lax.fori_loop(0, CHUNKS, backward, 0)
-
-    total_rows = CHUNKS * images * PIX
+    lax.fori_loop(0, chunks, backward, 0)
+
+    total_rows = chunks * rows
     flat_d = dconv[...].reshape(total_rows, chans)
 
     def grad_rows(k, _):
@@ -493,7 +514,7 @@
 
     lax.fori_loop(0, chans // 128, grad_rows, 0)
     inner = sq_ref.shape[1]
-    small = CHUNKS * pooled.shape[1]
+    small = chunks * pooled.shape[1]
     wg[:, chans : chans + inner] = outer_split(
         pooled[...].reshape(small, chans), du_s[...].reshape(small, inner)
     )
@@ -599,7 +620,7 @@
             def _(part=part, buf=buf, zz=zz):
                 ag_copy(part, buf, column(zz), 1, core).wait_send()
 
-    for j in range(CHUNKS):
+    for j in range(chunks):
 
         @pl.when(seg == 0)
         def _(j=j):
@@ -615,15 +636,13 @@
     micro, batch, height, width, chans = inputs.shape
     share, inner = squeeze_weight.shape[1:]
     zdim = fsdp // 4
-    images = micro * batch // CHUNKS
-    rows = images * PIX
+    positions = height * width
+    rows = -(-positions * micro // GRP) * GRP
     wide = -(-inner // 128) * 128
     cut = (chans // 128 + 1) // 2 * 128
-    narrow = -(-images // 8) * 8
-
-    def padded(arr):
-        arr = jnp.pad(arr, ((0, 0), (0, 0), (0, 8 - height), (0, 8 - width), (0, 0)))
-        return arr.reshape(CHUNKS, rows, chans)
+
+    def by_image(arr):
+        return arr.transpose(1, 2, 3, 0, 4).reshape(batch, positions, micro, chans)
 
     def widened(arr):
         return jnp.pad(arr, ((0, 0), (0, wide - inner)))
@@ -634,15 +653,15 @@
     vm = pl.BlockSpec(memory_space=pltpu.VMEM)
     v = pltpu.VMEM
     dma = pltpu.SemaphoreType.DMA
-    act = v((CHUNKS, rows, chans), BF16)
+    act = v((batch, rows, chans), BF16)
 
     def small(cols):
-        return v((CHUNKS, narrow, cols), F32)
+        return v((batch, 8, cols), F32)
 
     gout, pg, sg, eg = pl.pallas_call(
-        functools.partial(fused_kernel, (zdim, share, images)),
+        functools.partial(fused_kernel, (zdim, share)),
         out_shape=(
-            jax.ShapeDtypeStruct((CHUNKS, rows, chans), BF16),
+            jax.ShapeDtypeStruct((batch, rows, chans), BF16),
             jax.ShapeDtypeStruct((share, chans), F32),
             jax.ShapeDtypeStruct((share, wide), F32),
             jax.ShapeDtypeStruct((share, wide), F32),
@@ -653,9 +672,8 @@
             v((fsdp, share, ca), BF16), v((fsdp, share, cb), BF16),
             v((chans, chans), BF16), v((chans, wide), BF16), v((chans, wide), BF16),
             act, act, act,
-            v((CHUNKS, rows, chans), F32), v((rows, chans), F32), act,
-            small(chans), small(wide), small(chans),
-            v((narrow, chans), F32), v((narrow, chans), F32),
+            v((batch, rows, chans), F32), v((rows, chans), F32), act,
+            small(chans), small(wide), v((batch, GRP, chans), F32), v((GRP, chans), F32),
             small(wide), small(wide), small(chans),
             v((chans, chans + 2 * wide), F32),
             v((fsdp, share, ca), BF16), v((fsdp, share, cb), BF16),
@@ -664,11 +682,12 @@
             v((zdim, share, ca), BF16), v((zdim, share, cb), BF16),
             dma((2, 4, fsdp)), dma((2, fsdp)),
             dma((2, 4 * zdim)), dma((2, 4 * zdim)),
-            dma((2, CHUNKS)), dma((2, CHUNKS)),
+            dma((2, batch)), dma((2, batch)),
         ],
         compiler_params=pltpu.CompilerParams(collective_id=0, has_side_effects=True),
-    )(padded(inputs), padded(cotangent), part_a, part_b)
-    grads = gout.reshape(micro, batch, 8, 8, chans)[:, :, :height, :width]
+    )(by_image(inputs), by_image(cotangent), part_a, part_b)
+    grads = gout[:, : positions * micro].reshape(batch, height, width, micro, chans)
+    grads = grads.transpose(3, 0, 1, 2, 4)
     return grads[None], pg[None], sg[None, :, :inner], eg[:, :inner].T[None]
 
 

time: 93.9 us -> 89.8 us (0.956)
  local copies, waits for them, and re-layouts: 9.98 us -> 5.99 us
    unnamed x12 -> x7, local copies, waits for them, and re-layouts: 3.63 us -> 0.69 us
    pad x2 -> x0, local copies, waits for them, and re-layouts: 2.71 us -> none  [padded(): jnp.pad(arr, ((0, 0), (0, 0), (0, 8 - height), (0, 8 - width), (0, 0)))]
    reshape x0 -> x1, local copies, waits for them, and re-layouts: none -> 1.72 us  [fused_body(): gout[:, :positions * micro].reshape(batch, height, width, micro, chans)]
where the time goes in v2:
time: 89.8 us; the launch traced here: 89.4 us
  Pallas kernels  79.9 us (89%)
  local copies, waits for them, and re-layouts  5.99 us (7%)
  other arithmetic  2.78 us (3%)
    pallas_call x1, Pallas kernels, fused_body(): pl.pallas_call(functools.partial(fused_kernel, (zdim, share)), out_shape=...  79.9 us

profile of v2, /device:TPU:0, one launch (start us, length us, event | category | flops | bytes accessed | tf_op | source)
XLA Modules:
  0.0 89.4 jit_solution(3705000301466076243)
XLA Ops:
  0.6 0.8 slice_bitcast_fusion.3
  1.4 1.4 %fusion.3.b_ref = bf16[56,640]{1,0:T(8,128)(2,1)} fusion(bf16[56,224]{1,0:T(8,128)(2,1)} %bitcast.28, bf16[56,384]{1,0:T(8,128)(2,1)S(1)} %slice_bitcast_fusion.3), kind=kLoop, calls=%fused_computation.5 | loop fusion | flops 215040 | bytes 139776 | tf_op jit(solution)/shard_map/concatenate | solution.py:651
  2.8 0.8 slice_bitcast_fusion.2
  3.6 1.4 %fusion.2.a_ref = bf16[56,768]{1,0:T(8,128)(2,1)} fusion(bf16[56,224]{1,0:T(8,128)(2,1)} %bitcast.29, bf16[56,512]{1,0:T(8,128)(2,1)S(1)} %slice_bitcast_fusion.2), kind=kLoop, calls=%fused_computation.4 | loop fusion | flops 258048 | bytes 168448 | tf_op jit(solution)/shard_map/concatenate | solution.py:650
  5.0 79.9 %shard_map.84 = (bf16[3,208,896]{2,1,0:T(8,128)(2,1)}, f32[56,896]{1,0:T(8,128)}, f32[56,256]{1,0:T(8,128)}, f32[56,256]{1,0:T(8,128)}) custom-call(bf16[3,49,4,896]{3,2,1,0:T(4,128)(2,1)} %bitcast.24, bf16[3,49,4,896]{3,2,1,0:T(4,128)(2,1)} %bitcast.25, bf16[56,768]{1,0:T(8,128)(2,1)} %fusion.2.a_ref, bf16[56,640]{1,0:T(8,128)(2,1)} %fusion.3.b_ref), custom_call_target="tpu_custom_call" | custom-call | tf_op jit(solution)/shard_map/pallas_call | solution.py:661
  85.0 1.3 %slice.17 = bf16[3,196,896]{2,1,0:T(8,128)(2,1)S(1)} slice(bf16[3,208,896]{2,1,0:T(8,128)(2,1)} %get-tuple-element.8), slice={[0:3], [0:196], [0:896]} | slice | bytes 2107392 | tf_op jit(solution)/shard_map/slice | solution.py:689
  86.3 0.0 copy-start.1
  86.3 0.0 copy-start.2
  86.3 0.0 copy-start
  86.3 1.7 %reshape.19 = bf16[3,7,7,4,896]{4,3,2,1,0:T(4,128)(2,1)} reshape(bf16[3,196,896]{2,1,0:T(8,128)(2,1)S(1)} %slice.17) | data formatting | bytes 2107392 | tf_op jit(solution)/shard_map/reshape | solution.py:689
  88.0 0.0 copy-done.1
  88.0 0.0 copy-done.2
  88.0 0.6 slice_bitcast_fusion
  88.7 0.0 copy-done
  88.7 0.7 copy.10
Async XLA Ops:
  86.3 1.7 %copy-start.1 = (f32[56,256]{1,0:T(8,128)S(1)}, f32[56,256]{1,0:T(8,128)}, u32[]{:S(2)}) copy-start(f32[56,256]{1,0:T(8,128)} %get-tuple-element.10) | copy-start | bytes 172036
  86.3 1.7 %copy-start.2 = (f32[56,256]{1,0:T(8,128)S(1)}, f32[56,256]{1,0:T(8,128)}, u32[]{:S(2)}) copy-start(f32[56,256]{1,0:T(8,128)} %get-tuple-element.11) | copy-start | bytes 172036
  86.3 2.4 %copy-start = (f32[56,896]{1,0:T(8,128)S(1)}, f32[56,896]{1,0:T(8,128)}, u32[]{:S(2)}) copy-start(f32[56,896]{1,0:T(8,128)} %get-tuple-element.9) | copy-start | bytes 602116

commit v3 on v2

--- a/solution.py
+++ b/solution.py
@@ -227,8 +227,8 @@
 
 
 def fused_kernel(
-    size, x_ref, cot_ref, a_ref, b_ref, gout_ref, pg_ref, sg_ref, eg_ref,
-    ga, gb, w_ref, sq_ref, ex_ref, hbuf, hnext, dybuf, conv, dpb, dconv,
+    size, x_ref, cot_ref, p_ref, s_ref, e_ref, gout_ref, pg_ref, sg_ref, eg_ref,
+    a_ref, b_ref, gbuf, ga, gb, w_ref, sq_ref, ex_ref, hbuf, hnext, dybuf, conv, dpb, dconv,
     pooled, u_s, gate_s, dpool, z_s, du_s, dv_s, wg,
     sa, sb, rxa, rxb, rya, ryb, rza, rzb,
     ag_send, ag_recv, rs_send, rs_recv, relay_send, relay_recv,
@@ -247,6 +247,17 @@
     def place(zz, yy, xx):
         return (seg, zz * 4 + yy * 2 + xx)
 
+    inner = s_ref.shape[1]
+    a_ref[:, :cut] = p_ref[:, :cut]
+    a_ref[:, cut:] = jnp.zeros((share, a_ref.shape[1] - cut), BF16)
+    a_ref[:, cut : cut + inner] = s_ref[...]
+    rest = chans - cut
+    b_ref[:, :rest] = p_ref[:, cut:]
+    b_ref[:, rest:] = jnp.zeros((share, b_ref.shape[1] - rest), BF16)
+    b_ref[:, rest : rest + inner] = e_ref[...]
+    for _, buf, own in ((0, ga, a_ref), (1, gb, b_ref)):
+        buf[me] = own[...]
+
     barrier = pltpu.get_barrier_semaphore()
     pl.semaphore_signal(barrier, inc=1, device_id=core, device_id_type=MESH)
     pl.semaphore_signal(barrier, inc=1, device_id=place(z, y, 1 - x), device_id_type=MESH)
@@ -305,9 +316,6 @@
             ag_copy(part, buf, block, 1, place(down, y, x), own).start()
 
         spread(part, buf, z, own)
-    for _, buf, own in parts:
-        buf[me] = own[...]
-
     def rows_of(q):
         return pl.ds(pl.multiple_of(q * GRP, GRP), GRP)
 
@@ -459,7 +467,7 @@
     def backward(j, _):
         @pl.when(seg == 0)
         def _():
-            relay(gout_ref, dybuf, 1, j).wait_recv()
+            relay(gbuf, dybuf, 1, j).wait_recv()
 
         def slope(q, total):
             c = conv[j, rows_of(q), :]
@@ -491,11 +499,11 @@
         back = lax.dot_general(
             dconv[j], w_ref[...], (((1,), (1,)), ((), ())), preferred_element_type=F32
         )
-        gout_ref[j] = (dybuf[j].astype(F32) + back).astype(BF16)
+        gbuf[j] = (dybuf[j].astype(F32) + back).astype(BF16)
 
         @pl.when(seg == 1)
         def _():
-            relay(gout_ref, dybuf, 1, j).start()
+            relay(gbuf, dybuf, 1, j).start()
 
         return 0
 
@@ -513,20 +521,20 @@
         return 0
 
     lax.fori_loop(0, chans // 128, grad_rows, 0)
-    inner = sq_ref.shape[1]
+    wide = sq_ref.shape[1]
     small = chunks * pooled.shape[1]
-    wg[:, chans : chans + inner] = outer_split(
-        pooled[...].reshape(small, chans), du_s[...].reshape(small, inner)
-    )
-    wg[:, chans + inner :] = outer_split(
-        dv_s[...].reshape(small, chans), z_s[...].reshape(small, inner)
+    wg[:, chans : chans + wide] = outer_split(
+        pooled[...].reshape(small, chans), du_s[...].reshape(small, wide)
+    )
+    wg[:, chans + wide :] = outer_split(
+        dv_s[...].reshape(small, chans), z_s[...].reshape(small, wide)
     )
 
     def term(part, block):
-        rows = pl.ds(pl.multiple_of(block * share, 8), share)
+        at = pl.ds(pl.multiple_of(block * share, 8), share)
         if part == 0:
-            return wg[rows, :cut], wg[rows, chans : chans + inner]
-        return wg[rows, cut:chans], wg[rows, chans + inner :]
+            return wg[at, :cut], wg[at, chans : chans + wide]
+        return wg[at, cut:chans], wg[at, chans + wide :]
 
     rs = ((0, sa, rxa, rya, rza), (1, sb, rxb, ryb, rzb))
 
@@ -571,6 +579,25 @@
                 block, copy = one(part, stage, r1, k, side)
                 stage[block] = joined(part, block).astype(BF16)
                 copy.start()
+
+    def unload(j, _):
+        step = GRP // micro
+
+        def group(q, _):
+            val = gbuf[j, rows_of(q), :].astype(F32)
+            for t in range(step):
+                gout_ref[j, q * step + t] = val[t * micro : (t + 1) * micro].astype(BF16)
+            return 0
+
+        lax.fori_loop(0, positions // step, group, 0)
+        for p in range(positions // step * step, positions):
+            val = gbuf[j, p * micro // GRP * GRP : (p * micro // GRP + 1) * GRP, :].astype(F32)
+            off = p * micro % GRP
+            gout_ref[j, p] = val[off : off + micro].astype(BF16)
+        return 0
+
+    lax.fori_loop(0, chunks, unload, 0)
+
     for k in range(zdim):
         for part, stage, r1, r2, r3 in rs:
             one(part, stage, r1, k, 0)[1].wait_recv()
@@ -594,10 +621,10 @@
             value = value + r3[k].astype(F32)
         if part == 0:
             pg_ref[:, :cut] = value[:, :cut]
-            sg_ref[...] = value[:, cut:]
+            sg_ref[...] = value[:, cut : cut + inner]
         else:
             pg_ref[:, cut:] = value[:, : chans - cut]
-            eg_ref[...] = value[:, chans - cut :]
+            eg_ref[...] = value[:, rest : rest + inner]
 
     for part, stage, r1, r2, r3 in rs:
         for k in range(zdim):
@@ -628,7 +655,7 @@
 
         @pl.when(seg == 1)
         def _(j=j):
-            relay(gout_ref, dybuf, 1, j).wait_send()
+            relay(gbuf, dybuf, 1, j).wait_send()
 
 
 def fused_body(inputs, cotangent, proj, squeeze_weight, excite_weight):
@@ -644,12 +671,7 @@
     def by_image(arr):
         return arr.transpose(1, 2, 3, 0, 4).reshape(batch, positions, micro, chans)
 
-    def widened(arr):
-        return jnp.pad(arr, ((0, 0), (0, wide - inner)))
-
-    part_a = jnp.concatenate([proj[0, :, :cut], widened(squeeze_weight[0])], 1)
-    part_b = jnp.concatenate([proj[0, :, cut:], widened(excite_weight[0].T)], 1)
-    ca, cb = part_a.shape[1], part_b.shape[1]
+    ca, cb = cut + wide, chans - cut + wide
     vm = pl.BlockSpec(memory_space=pltpu.VMEM)
     v = pltpu.VMEM
     dma = pltpu.SemaphoreType.DMA
@@ -661,14 +683,15 @@
     gout, pg, sg, eg = pl.pallas_call(
         functools.partial(fused_kernel, (zdim, share)),
         out_shape=(
-            jax.ShapeDtypeStruct((batch, rows, chans), BF16),
+            jax.ShapeDtypeStruct((batch, positions, micro, chans), BF16),
             jax.ShapeDtypeStruct((share, chans), F32),
-            jax.ShapeDtypeStruct((share, wide), F32),
-            jax.ShapeDtypeStruct((share, wide), F32),
+            jax.ShapeDtypeStruct((share, inner), F32),
+            jax.ShapeDtypeStruct((share, inner), F32),
         ),
-        in_specs=[vm] * 4,
+        in_specs=[vm] * 5,
         out_specs=(vm,) * 4,
         scratch_shapes=[
+            v((share, ca), BF16), v((share, cb), BF16), act,
             v((fsdp, share, ca), BF16), v((fsdp, share, cb), BF16),
             v((chans, chans), BF16), v((chans, wide), BF16), v((chans, wide), BF16),
             act, act, act,
@@ -685,10 +708,10 @@
             dma((2, batch)), dma((2, batch)),
         ],
         compiler_params=pltpu.CompilerParams(collective_id=0, has_side_effects=True),
-    )(by_image(inputs), by_image(cotangent), part_a, part_b)
-    grads = gout[:, : positions * micro].reshape(batch, height, width, micro, chans)
+    )(by_image(inputs), by_image(cotangent), proj[0], squeeze_weight[0], excite_weight[0].T)
+    grads = gout.reshape(batch, height, width, micro, chans)
     grads = grads.transpose(3, 0, 1, 2, 4)
-    return grads[None], pg[None], sg[None, :, :inner], eg[:, :inner].T[None]
+    return grads[None], pg[None], sg[None], eg.T[None]
 
 
 def suits(mesh):

time: 89.8 us -> 85.4 us (0.951)
  other arithmetic: 2.78 us -> 0 us
  local copies, waits for them, and re-layouts: 5.99 us -> 4.54 us
    unnamed x7 -> x10, local copies, waits for them, and re-layouts: 0.69 us -> 4.54 us
    concatenate x2 -> x0, other arithmetic: 2.78 us -> none  [the longest x1 1.39 us: fused_body(): part_a = jnp.concatenate([proj[0, :, :cut], widened(squeeze_weight[0])], 1)]
    reshape x1 -> x0, local copies, waits for them, and re-layouts: 1.72 us -> none  [fused_body(): gout[:, :positions * micro].reshape(batch, height, width, micro, chans)]
    squeeze x2 -> x0, local copies, waits for them, and re-layouts: 1.61 us -> none  [the longest x1 0.82 us: fused_body(): part_a = jnp.concatenate([proj[0, :, :cut], widened(squeeze_weight[0])], 1)]
    slice x1 -> x0, local copies, waits for them, and re-layouts: 1.33 us -> none  [fused_body(): gout[:, :positions * micro].reshape(batch, height, width, micro, chans)]
where the time goes in v3:
time: 85.4 us; the launch traced here: 85.3 us
  Pallas kernels  80.1 us (94%)
  local copies, waits for them, and re-layouts  4.54 us (5%)
    pallas_call x1, Pallas kernels, fused_body(): pl.pallas_call(functools.partial(fused_kernel, (zdim, share)), out_shape=...  80.1 us
    unnamed x10, local copies, waits for them, and re-layouts  4.54 us

profile of v3, /device:TPU:0, one launch (start us, length us, event | category | flops | bytes accessed | tf_op | source)
XLA Modules:
  0.0 85.3 jit_solution(1100663750403234187)
XLA Ops:
  0.6 80.1 %shard_map.84 = (bf16[3,49,4,896]{3,2,1,0:T(4,128)(2,1)}, f32[56,896]{1,0:T(8,128)}, f32[56,224]{1,0:T(8,128)}, f32[56,224]{1,0:T(8,128)}) custom-call(bf16[3,49,4,896]{3,2,1,0:T(4,128)(2,1)} %bitcast.21, bf16[3,49,4,896]{3,2,1,0:T(4,128)(2,1)} %bitcast.22, bf16[56,896]{1,0:T(8,128)(2,1)} %bitcast.25, bf16[56,224]{1,0:T(8,128)(2,1)} %bitcast.28, ...), custom_call_target="tpu_custom_call" | custom-call | tf_op jit(solution)/shard_map/pallas_call | solution.py:683
  80.7 0.0 copy-start
  80.7 0.0 copy-start.2
  80.7 0.0 copy-start.1
  80.7 2.6 %copy.13 = bf16[1,4,3,7,7,896]{5,1,4,3,2,0:T(4,128)(2,1)} copy(bf16[1,4,3,7,7,896]{5,1,4,3,2,0:T(4,128)(2,1)} %bitcast.23) | data formatting | bytes 2107392
  83.3 0.0 copy-done
  83.3 0.7 copy.14
  84.0 0.0 copy-done.2
  84.0 0.6 copy.15
  84.6 0.0 copy-done.1
  84.7 0.6 copy.16
Async XLA Ops:
  80.7 2.6 %copy-start = (f32[56,896]{1,0:T(8,128)S(1)}, f32[56,896]{1,0:T(8,128)}, u32[]{:S(2)}) copy-start(f32[56,896]{1,0:T(8,128)} %get-tuple-element.9) | copy-start | bytes 602116
  80.7 3.3 %copy-start.2 = (f32[56,224]{1,0:T(8,128)S(1)}, f32[56,224]{1,0:T(8,128)}, u32[]{:S(2)}) copy-start(f32[56,224]{1,0:T(8,128)} %get-tuple-element.10) | copy-start | bytes 150532
  80.7 3.9 %copy-start.1 = (f32[56,224]{1,0:T(8,128)S(1)}, f32[56,224]{1,0:T(8,128)}, u32[]{:S(2)}) copy-start(f32[56,224]{1,0:T(8,128)} %get-tuple-element.11) | copy-start | bytes 150532

commit v4 on v3

--- a/solution.py
+++ b/solution.py
@@ -227,7 +227,7 @@
 
 
 def fused_kernel(
-    size, x_ref, cot_ref, p_ref, s_ref, e_ref, gout_ref, pg_ref, sg_ref, eg_ref,
+    size, x_ref, cot_ref, p_ref, s_ref, e_ref, gout_ref, wg_ref,
     a_ref, b_ref, gbuf, ga, gb, w_ref, sq_ref, ex_ref, hbuf, hnext, dybuf, conv, dpb, dconv,
     pooled, u_s, gate_s, dpool, z_s, du_s, dv_s, wg,
     sa, sb, rxa, rxb, rya, ryb, rza, rzb,
@@ -620,11 +620,11 @@
             three(part, stage, r3, k)[1].wait_recv()
             value = value + r3[k].astype(F32)
         if part == 0:
-            pg_ref[:, :cut] = value[:, :cut]
-            sg_ref[...] = value[:, cut : cut + inner]
+            wg_ref[:, :cut] = value[:, :cut]
+            wg_ref[:, chans : chans + wide] = value[:, cut:]
         else:
-            pg_ref[:, cut:] = value[:, : chans - cut]
-            eg_ref[...] = value[:, rest : rest + inner]
+            wg_ref[:, cut:chans] = value[:, :rest]
+            wg_ref[:, chans + wide :] = value[:, rest:]
 
     for part, stage, r1, r2, r3 in rs:
         for k in range(zdim):
@@ -680,16 +680,14 @@
     def small(cols):
         return v((batch, 8, cols), F32)
 
-    gout, pg, sg, eg = pl.pallas_call(
+    gout, terms = pl.pallas_call(
         functools.partial(fused_kernel, (zdim, share)),
         out_shape=(
             jax.ShapeDtypeStruct((batch, positions, micro, chans), BF16),
-            jax.ShapeDtypeStruct((share, chans), F32),
-            jax.ShapeDtypeStruct((share, inner), F32),
-            jax.ShapeDtypeStruct((share, inner), F32),
+            jax.ShapeDtypeStruct((share, chans + 2 * wide), F32),
         ),
         in_specs=[vm] * 5,
-        out_specs=(vm,) * 4,
+        out_specs=(vm,) * 2,
         scratch_shapes=[
             v((share, ca), BF16), v((share, cb), BF16), act,
             v((fsdp, share, ca), BF16), v((fsdp, share, cb), BF16),
@@ -711,7 +709,9 @@
     )(by_image(inputs), by_image(cotangent), proj[0], squeeze_weight[0], excite_weight[0].T)
     grads = gout.reshape(batch, height, width, micro, chans)
     grads = grads.transpose(3, 0, 1, 2, 4)
-    return grads[None], pg[None], sg[None], eg.T[None]
+    at = chans + wide
+    sg, eg = terms[:, chans : chans + inner], terms[:, at : at + inner]
+    return grads[None], terms[None, :, :chans], sg[None], eg.T[None]
 
 
 def suits(mesh):

time: 85.4 us -> 86.6 us (1.014)
  local copies, waits for them, and re-layouts: 4.54 us -> 5.67 us
    broadcast_in_dim x0 -> x2, local copies, waits for them, and re-layouts: none -> 3.11 us  [fused_body(): return (grads[None], terms[None, :, :chans], sg[None], eg.T[None])]
    unnamed x10 -> x1, local copies, waits for them, and re-layouts: 4.54 us -> 2.56 us
where the time goes in v4:
time: 86.6 us; the launch traced here: 86.4 us
  Pallas kernels  80 us (92%)
  local copies, waits for them, and re-layouts  5.67 us (7%)
    pallas_call x1, Pallas kernels, fused_body(): pl.pallas_call(functools.partial(fused_kernel, (zdim, share)), out_shape=...  80 us
    broadcast_in_dim x2, local copies, waits for them, and re-layouts, fused_body(): return (grads[None], terms[None, :, :chans], sg[None], eg.T[None])  3.11 us
    unnamed x1, local copies, waits for them, and re-layouts  2.56 us

profile of v4, /device:TPU:0, one launch (start us, length us, event | category | flops | bytes accessed | tf_op | source)
XLA Modules:
  0.0 86.4 jit_solution(14105494900309290194)
XLA Ops:
  0.6 80.0 %shard_map.84 = (bf16[3,49,4,896]{3,2,1,0:T(4,128)(2,1)}, f32[56,1408]{1,0:T(8,128)}) custom-call(bf16[3,49,4,896]{3,2,1,0:T(4,128)(2,1)} %bitcast.24, bf16[3,49,4,896]{3,2,1,0:T(4,128)(2,1)} %bitcast.25, bf16[56,896]{1,0:T(8,128)(2,1)} %bitcast.27, bf16[56,224]{1,0:T(8,128)(2,1)} %bitcast.28, bf16[56,224]{1,0:T(8,128)(2,1)} %bitcast.29), custom_call_target="tpu_custom_call" | custom-call | tf_op jit(solution)/shard_map/pallas_call | solution.py:683
  80.7 1.5 %slice_bitcast_fusion.1 = (f32[1,224,56]{1,2,0:T(8,128)}, f32[1,56,224]{2,1,0:T(8,128)}) fusion(f32[56,1408]{1,0:T(8,128)} %get-tuple-element.7), kind=kLoop, calls=%fused_computation.1 | loop fusion | bytes 200704 | tf_op jit(solution)/shard_map/broadcast_in_dim | solution.py:714
  82.2 1.6 %slice_bitcast_fusion = f32[1,56,896]{2,1,0:T(8,128)} fusion(f32[56,1408]{1,0:T(8,128)} %get-tuple-element.7), kind=kLoop, calls=%fused_computation | loop fusion | bytes 401408 | tf_op jit(solution)/shard_map/broadcast_in_dim | solution.py:714
  83.8 2.6 %copy.10 = bf16[1,4,3,7,7,896]{5,1,4,3,2,0:T(4,128)(2,1)} copy(bf16[1,4,3,7,7,896]{5,1,4,3,2,0:T(4,128)(2,1)} %bitcast.26) | data formatting | bytes 2107392
